TPU v7x, 32 devices: a whole 2x2x4 slice. The times are simulated.
32 devices in a mesh: px: 8 (over z, y), py: 4 (over x, core).
Axes of the slice: x: 2, y: 2, z: 4, core: 2. Of those that a mesh axis runs over, the one named last changes fastest.
Arguments:
- point_channel_values: bfloat16 [4096, 64, 128], P(('px', 'py')), may hold values from -6 to 6
- point_offsets: bfloat16 [4096, 3, 128], P(('px', 'py')), may hold values from -1 to 17
- point_counts: int32 [4096], P(('px', 'py')), may hold values from 1 to 128
- block_bricks: int32 [4096, 4], P(('px', 'py')), may hold values from 0 to 16383, as said below
- spectral_weights: bfloat16 [2, 32, 32, 32, 64, 128], P(None, None, 'px', 'py'), may hold values from -0.5 to 0.5
- skip_weights: bfloat16 [2, 64, 64], replicated, may hold values from -0.75 to 0.75
- skip_bias: float32 [2, 64], replicated, may hold values from -3 to 3
Outputs:
- decoded: bfloat16 [4096, 64, 128], P(('px', 'py'))
Inputs may be any that keep to these rules, and one draw needn't show every extreme that they name: `block_bricks`: the 4 bricks of a block are distinct and lie on one device. Among the 128 blocks of one device at most 8 have their bricks on any one device, and in every draw some device receives exactly 8 blocks from every device.
All inputs are finite; a program needn't handle non-finite values.
Results may differ from a plain program's by a relative error of at most 0.0075.
Values may be sent and summed in bfloat16 or wider, within the bound.
A program may use at most 256 MiB of HBM per device.

v0:
```python
import math
import jax
import jax.numpy as jnp
from jax import lax
from jax.sharding import PartitionSpec as P

MODES = 32
NX = 128
NY = 128
NZ = 128
LAYERS = 2
AMPLITUDE = 0.25
SPREAD = 4.5
DECODE_SCALE = 0.1
PRECISE = lax.Precision.HIGHEST


def wave_numbers(kept_modes):
    position = jnp.arange(kept_modes, dtype=jnp.int32)
    return jnp.where(position < kept_modes // 2, position, position - kept_modes)


def forward_matrix(length, frequency):
    places = jnp.arange(length, dtype=jnp.int32)
    products = jnp.remainder(places[:, None] * frequency[None, :], length)
    angles = 2.0 * math.pi / length * products.astype(jnp.float32)
    cosine = jnp.cos(angles) / math.sqrt(length)
    sine_part = jnp.sin(angles) / math.sqrt(length)
    from_real = jnp.stack([cosine, -sine_part], axis=-1)
    from_imag = jnp.stack([sine_part, cosine], axis=-1)
    return jnp.stack([from_real, from_imag], axis=1)


def cell_centers():
    cell_index = jnp.arange(128, dtype=jnp.int32)
    return (
        jnp.stack([cell_index // 64, cell_index // 16 % 4, cell_index % 16]).astype(jnp.float32)
        + 0.5
    )


def brick_anchor(local_ids, bricks_y, bricks_z):
    clamped_weights = jnp.maximum(local_ids, 0)
    return jnp.stack(
        [
            2 * (clamped_weights // (bricks_y * bricks_z)),
            4 * (clamped_weights // bricks_z % bricks_y),
            16 * (clamped_weights % bricks_z),
        ],
        axis=-1,
    ).astype(jnp.float32)


def block_work(features, offsets, counts, local_ids, bricks_y, bricks_z):
    total_items, channels, points = features.shape
    group_size = math.gcd(total_items, 16)
    centers = cell_centers()

    def one_group(items):
        feature_share, offset_part, count_part, id_part = items
        validity = (jnp.arange(points, dtype=jnp.int32)[None, :] < count_part[:, None]).astype(
            jnp.float32
        )
        anchors = brick_anchor(id_part, bricks_y, bricks_z)
        relative_position = anchors - anchors[:, :1, :]
        placed = offset_part.astype(jnp.float32)[:, None, :, :] - relative_position[:, :, :, None]
        apart = placed[..., None] - centers[None, None, :, None, :]
        distance = jnp.sum(apart * apart, axis=2)
        kernel_weight_value = (
            AMPLITUDE * jnp.exp(-distance / SPREAD) * validity[:, None, :, None]
        ).astype(jnp.bfloat16)
        brick_tile_grid = jnp.einsum(
            "dqw,dewn->deqn", feature_share, kernel_weight_value, preferred_element_type=jnp.float32
        ).astype(jnp.bfloat16)
        return (kernel_weight_value, brick_tile_grid)

    grouped = tuple(
        (
            member.reshape((total_items // group_size, group_size) + member.shape[1:])
            for member in (features, offsets, counts, local_ids)
        )
    )
    kernel_weight_value, brick_tile_grid = lax.map(one_group, grouped)
    return (
        kernel_weight_value.reshape((total_items,) + kernel_weight_value.shape[2:]),
        brick_tile_grid.reshape((total_items,) + brick_tile_grid.shape[2:]),
    )


def decode_points(brick_values, kernel_weight_value):
    summed = jnp.einsum(
        "nhcx,nhpx->ncp", brick_values, kernel_weight_value, preferred_element_type=jnp.float32
    )
    return (DECODE_SCALE * summed).astype(jnp.bfloat16)


def accumulate(brick_tile_grid, local_ids, bricks_device):
    flat_ids = local_ids.reshape(-1)
    selector = (flat_ids[:, None] == jnp.arange(bricks_device, dtype=jnp.int32)[None, :]).astype(
        jnp.bfloat16
    )
    flat_tiles = brick_tile_grid.reshape((flat_ids.shape[0],) + brick_tile_grid.shape[2:])
    return jnp.einsum("rb,rcx->bcx", selector, flat_tiles, preferred_element_type=jnp.float32)


def to_grid(bricks, bricks_along_first, bricks_y, bricks_z):
    channels = bricks.shape[1]
    shaped = bricks.reshape(bricks_along_first, bricks_y, bricks_z, channels, 2, 4, 16)
    return shaped.transpose(3, 0, 4, 1, 5, 2, 6).reshape(
        channels, 2 * bricks_along_first, 4 * bricks_y, 16 * bricks_z
    )


def to_bricks(grid, bricks_along_first, bricks_y, bricks_z):
    channels = grid.shape[0]
    shaped = grid.reshape(channels, bricks_along_first, 2, bricks_y, 4, bricks_z, 16)
    return shaped.transpose(1, 3, 5, 0, 2, 4, 6).reshape(
        bricks_along_first * bricks_y * bricks_z, channels, 128
    )


def spectral(grid, weights, tables):
    table_third, forward_second, forward_first, back_second, back_first, back_third = tables
    channels, cells_x = (grid.shape[0], grid.shape[1])
    third_modes = jnp.einsum(
        "cxyz,zq->cxyq", grid.astype(jnp.float32), table_third, precision=PRECISE
    ).astype(jnp.bfloat16)
    columns = lax.all_to_all(third_modes, "py", split_axis=3, concat_axis=2, tiled=True)
    third_local = columns.shape[3] // 2
    second_modes = jnp.einsum(
        "cxyzp,ypkq->cxzkq",
        columns.reshape(channels, cells_x, columns.shape[2], third_local, 2).astype(jnp.float32),
        forward_second,
        precision=PRECISE,
    ).astype(jnp.bfloat16)
    row_lines = lax.all_to_all(second_modes, "px", split_axis=3, concat_axis=1, tiled=True)
    first_modes = jnp.einsum(
        "cxzkp,xpmq->mkzcq", row_lines.astype(jnp.float32), forward_first, precision=PRECISE
    ).astype(jnp.bfloat16)
    product = jnp.einsum(
        "mkzcp,mkzcr->mkzpr", first_modes, weights, preferred_element_type=jnp.float32
    )
    product = product.reshape(product.shape[:4] + (2, channels))
    mixed_real = product[:, :, :, 0, 0] - product[:, :, :, 1, 1]
    mixed_imag = product[:, :, :, 0, 1] + product[:, :, :, 1, 0]
    mixed = jnp.stack([mixed_real, mixed_imag], axis=-1)
    first_back = jnp.einsum("mkzcp,mpxq->cxzkq", mixed, back_first, precision=PRECISE).astype(
        jnp.bfloat16
    )
    row_back = lax.all_to_all(first_back, "px", split_axis=1, concat_axis=3, tiled=True)
    second_back = jnp.einsum(
        "cxzkp,kpyq->cxyzq", row_back.astype(jnp.float32), back_second, precision=PRECISE
    )
    second_back = second_back.reshape(channels, cells_x, second_back.shape[2], -1).astype(
        jnp.bfloat16
    )
    column_back = lax.all_to_all(second_back, "py", split_axis=2, concat_axis=3, tiled=True)
    return jnp.einsum(
        "cxyq,qz->cxyz", column_back.astype(jnp.float32), back_third, precision=PRECISE
    )


def slot_plan(block_bricks, bricks_device, slot_total, capacity):
    owners = block_bricks[:, 0] // bricks_device
    order_index = jnp.arange(owners.shape[0], dtype=jnp.int32)
    earlier = (owners[None, :] == owners[:, None]) & (order_index[None, :] < order_index[:, None])
    ranking = jnp.sum(earlier.astype(jnp.int32), axis=1)
    slot_index = owners * capacity + ranking
    matching = slot_index[None, :] == jnp.arange(slot_total, dtype=jnp.int32)[:, None]
    present = jnp.any(matching, axis=1)
    sources = jnp.sum(jnp.where(matching, order_index[None, :], 0), axis=1)
    return (slot_index, present, sources)


def pack_slots(values, present, sources, filler):
    picked = jnp.take(values, sources, axis=0)
    masking = present.reshape((-1,) + (1,) * (values.ndim - 1))
    return jnp.where(masking, picked, jnp.asarray(filler, values.dtype))


def route_back(values):
    return lax.all_to_all(values, ("px", "py"), split_axis=0, concat_axis=0, tiled=True)


def per_device(
    point_channel_values,
    point_offsets,
    point_counts,
    block_bricks,
    spectral_weights,
    skip_weights,
    skip_bias,
):
    mesh_rows = lax.axis_size("px")
    mesh_columns = lax.axis_size("py")
    device_total = mesh_rows * mesh_columns
    capacity = max(2, 2 * point_channel_values.shape[0] // device_total)
    bricks_along_first = NX // mesh_rows // 2
    bricks_y = NY // mesh_columns // 4
    bricks_z = NZ // 16
    bricks_device = bricks_along_first * bricks_y * bricks_z
    slot_total = device_total * capacity
    local_ids = block_bricks % bricks_device
    slot_index, present, sources = slot_plan(block_bricks, bricks_device, slot_total, capacity)
    packed_ids = pack_slots(local_ids, present, sources, -1)
    packed_features = pack_slots(point_channel_values, present, sources, 0)
    packed_offsets = pack_slots(point_offsets, present, sources, 0)
    packed_counts = pack_slots(point_counts, present, sources, 0)
    got_features, got_offsets, got_counts, got_ids = (
        lax.all_to_all(packed_features, ("px", "py"), split_axis=0, concat_axis=0, tiled=True),
        lax.all_to_all(packed_offsets, ("px", "py"), split_axis=0, concat_axis=0, tiled=True),
        lax.all_to_all(packed_counts, ("px", "py"), split_axis=0, concat_axis=0, tiled=True),
        lax.all_to_all(packed_ids, ("px", "py"), split_axis=0, concat_axis=0, tiled=True),
    )
    got_weight, got_tiles = block_work(
        got_features, got_offsets, got_counts, got_ids, bricks_y, bricks_z
    )
    encoded = accumulate(got_tiles, got_ids, bricks_device).astype(jnp.bfloat16)
    grid = to_grid(encoded, bricks_along_first, bricks_y, bricks_z)
    third_matrix = forward_matrix(NZ, jnp.arange(MODES, dtype=jnp.int32))[:, 0]
    weighting = jnp.where(jnp.arange(MODES) == 0, 1.0, 2.0).astype(jnp.float32)
    forward_second = forward_matrix(NY, wave_numbers(MODES))
    forward_first = forward_matrix(NX, wave_numbers(MODES))
    tables = (
        third_matrix.reshape(NZ, 2 * MODES),
        forward_second,
        forward_first,
        forward_second.transpose(2, 3, 0, 1),
        forward_first.transpose(2, 3, 0, 1),
        (third_matrix * weighting[None, :, None]).reshape(NZ, 2 * MODES).T,
    )
    for depth_index in range(LAYERS):
        spectral_part = spectral(grid, spectral_weights[depth_index], tables)
        skipped = jnp.einsum(
            "io,ixyz->oxyz", skip_weights[depth_index], grid, preferred_element_type=jnp.float32
        )
        grid = jax.nn.gelu(
            spectral_part + skipped + skip_bias[depth_index][:, None, None, None], approximate=False
        ).astype(jnp.bfloat16)
    final_bricks = to_bricks(grid, bricks_along_first, bricks_y, bricks_z)
    wanted = jnp.take(final_bricks, jnp.maximum(got_ids, 0), axis=0)
    reply = decode_points(wanted, got_weight)
    returned = route_back(reply)
    return jnp.take(returned, slot_index, axis=0)


def solution(mesh):
    return jax.shard_map(
        per_device,
        mesh=mesh,
        in_specs=(
            P(("px", "py"), None, None),
            P(("px", "py"), None, None),
            P(("px", "py")),
            P(("px", "py"), None),
            P(None, None, "px", "py", None, None),
            P(),
            P(),
        ),
        out_specs=P(("px", "py"), None, None),
        check_vma=False,
    )
```

profile of v0, /device:TPU:0, one launch (start us, length us, event | category | flops | bytes accessed | tf_op | source)
XLA Modules:
  0.0 1413.8 jit_solution(9622906543560222130)
XLA Ops:
  5.5 7.3 all-to-all-start.2
  19.9 4.5 all-to-all-start
  34.5 4.4 select_select_fusion
  38.9 6.2 all-to-all-done.1
  50.8 91.7 %all-to-all-done.3 = bf16[256,64,128]{2,1,0:T(8,128)(2,1)} async-done(((bf16[256,64,128]{2,1,0:T(8,128)(2,1)}), bf16[256,64,128]{2,1,0:T(8,128)(2,1)}, u32[]{:S(2)}, u32[]{:S(2)}) %all-to-all-start.3) | async-done | bytes 4194336 | tf_op jit(solution)/shard_map/all_to_all | solution.py:210
  142.5 154.9 %while.15 = (s32[]{:T(128)}, bf16[16,16,4,128,128]{4,3,2,1,0:T(8,128)(2,1)}, bf16[16,16,4,64,128]{4,3,2,1,0:T(8,128)(2,1)}, bf16[16,16,3,128]{3,2,1,0:T(4,128)(2...) while((s32[]{:T(128)}, ...), condition=%wide.region_5.6_spmd, body=%wide.region_3.5_spmd.sunk | while | flops 151557504 | bytes 16284649 | solution.py:83
  171.8 4.1 multiply_reduce_fusion.2
  297.4 30.3 %fusion.59 = bf16[512,64,128]{2,0,1:T(8,128)(2,1)} fusion(bf16[1024,64,128]{2,1,0:T(8,128)(2,1)} %bitcast.395, s32[1024]{0:T(1024)S(1)} %eq.74), kind=kOutput, calls=%fused_computation.116 | convolution fusion | flops 8594653184 | bytes 25169920 | tf_op jit(solution)/shard_map/rb,rcx->bcx/dot_general | solution.py:103
  327.7 17.6 %copy.421 = bf16[512,64,128]{1,2,0:T(8,128)(2,1)} copy(bf16[512,64,128]{2,0,1:T(8,128)(2,1)} %fusion.59) | data formatting | bytes 16777216 | tf_op jit(solution)/shard_map/convert_element_type | solution.py:218
  345.4 15.1 %copy.422 = bf16[64,8,2,8,4,8,16]{0,6,5,4,3,2,1:T(8,128)(2,1)} copy(bf16[64,8,2,8,4,8,16]{0,6,4,2,5,3,1:T(8,128)(2,1)} %bitcast.354) | data formatting | bytes 16777216 | tf_op jit(solution)/shard_map/transpose | solution.py:109
  360.5 18.9 %copy.424 = bf16[64,16,32,128]{3,2,1,0:T(8,128)(2,1)} copy(bf16[64,16,32,128]{0,3,2,1:T(8,128)(2,1)} %bitcast.350) | data formatting | bytes 16777216 | tf_op jit(solution)/shard_map/reshape | solution.py:109
  379.3 11.1 convolution_convert_fusion.1
  390.4 16.4 %copy.425 = bf16[64,16,32,64]{0,2,1,3:T(8,128)(2,1)} copy(bf16[64,16,32,64]{3,2,1,0:T(8,128)(2,1)} %convolution_convert_fusion.1) | data formatting | bytes 8388608 | tf_op jit(solution)/shard_map/convert_element_type | solution.py:127
  406.8 9.5 reshape.1014
  416.3 5.1 all-to-all-start.4
  421.6 48.0 %all-to-all-done.4 = bf16[4,2,262144]{2,1,0:T(2,128)(2,1)} async-done(((bf16[4,2,262144]{2,1,0:T(2,128)(2,1)}), bf16[4,2,262144]{2,1,0:T(2,128)(2,1)}, u32[]{:S(2)}, u32[]{:S(2)}) %all-to-all-start.4) | async-done | bytes 4194336 | tf_op jit(solution)/shard_map/all_to_all | solution.py:128
  469.6 9.3 reshape.1015
  478.9 9.3 copy.427
  488.1 10.1 copy.484
  498.2 10.3 bitcast_convert_fusion.4
  508.6 7.7 copy.429
  517.9 29.3 %all_to_all.165 = bf16[8,2,32768]{2,1,0:T(2,128)(2,1)} all-to-all(bf16[8,2,32768]{2,1,0:T(2,128)(2,1)S(1)} %reshape.1016), channel_id=1, replica_groups=mesh['px'=8,'py'=4] {'px'}, dimensions={0} | all-to-all | bytes 2097152 | tf_op jit(solution)/shard_map/all_to_all | solution.py:136
  557.1 8.1 fusion.32
  577.3 28.8 %all_to_all.166 = bf16[8,2,32768]{2,1,0:T(2,128)(2,1)S(1)} all-to-all(bf16[8,2,32768]{2,1,0:T(2,128)(2,1)S(1)} %reshape.1018), channel_id=1, replica_groups=mesh['px'=8,'py'=4] {'px'}, dimensions={0} | all-to-all | bytes 2097152 | tf_op jit(solution)/shard_map/all_to_all | solution.py:150
  615.3 4.6 copy.443
  619.9 16.5 %copy.444 = bf16[64,16,128,16]{0,3,1,2:T(8,128)(2,1)} copy(bf16[64,16,128,16]{2,1,3,0:T(8,128)(2,1)} %bitcast.368) | data formatting | bytes 8388608 | tf_op jit(solution)/shard_map/convert_element_type | solution.py:154
  636.4 9.6 reshape.1020
  646.0 5.1 all-to-all-start.7
  651.1 12.8 fusion.106
  663.9 35.3 %all-to-all-done.7 = bf16[4,2,262144]{2,1,0:T(2,128)(2,1)} async-done(((bf16[4,2,262144]{2,1,0:T(2,128)(2,1)}), bf16[4,2,262144]{2,1,0:T(2,128)(2,1)}, u32[]{:S(2)}, u32[]{:S(2)}) %all-to-all-start.7) | async-done | bytes 4194336 | tf_op jit(solution)/shard_map/all_to_all | solution.py:157
  699.2 9.3 reshape.1021
  708.5 9.1 copy.446
  717.6 13.1 copy.448
  730.7 28.6 %fusion.54 = (u16[64,32,128]{2,1,0:T(8,128)(2,1)S(1)}, f32[64,16,32,128]{3,2,1,0:T(8,128)}) fusion(f32[64]{0:T(128)S(1)} %get-tuple-element.225, f32[16,32,128,64]{2,3,1,0:T(8,128)} %fusion.106, bf16[64,16,32,64]{3,2,1,0:T(8,128)(2,1)} %copy.448, f32[128,64,1,1]{0,1,3,2:T(8,128)S(1)} %bitcast.388), kind=kOutput, calls=%fused_computation.104 | convolution fusion | flops 3258712064 | bytes 38306048 | tf_op jit(solution)/shard_map/cxyq,qz->cxyz/dot_general | solution.py:158
  759.3 38.4 %fusion.24 = bf16[64,16,32,128]{3,2,1,0:T(8,128)(2,1)S(1)} fusion(f32[64,16,32,128]{3,2,1,0:T(8,128)} %get-tuple-element.230, u16[64,32,128]{2,1,0:T(8,128)(2,1)S(1)} %get-tuple-element.229), kind=kLoop, calls=%fused_computation.54 | loop fusion | flops 285212672 | bytes 25690112 | tf_op jit(solution)/shard_map/convert_element_type | solution.py:239
  801.0 8.6 convolution_convert_fusion
  809.6 16.4 %copy.452 = bf16[64,16,32,64]{0,2,1,3:T(8,128)(2,1)} copy(bf16[64,16,32,64]{3,2,1,0:T(8,128)(2,1)} %convolution_convert_fusion) | data formatting | bytes 8388608 | tf_op jit(solution)/shard_map/convert_element_type | solution.py:127
  826.0 9.5 reshape.1022
  835.5 54.0 %all_to_all.167 = bf16[4,2,262144]{2,1,0:T(2,128)(2,1)} all-to-all(bf16[4,2,262144]{2,1,0:T(2,128)(2,1)} %reshape.1022), channel_id=1, replica_groups=mesh['px'=8,'py'=4] {'py'}, dimensions={0} | all-to-all | bytes 8388608 | tf_op jit(solution)/shard_map/all_to_all | solution.py:128
  889.5 9.3 reshape.1023
  898.8 9.3 copy.454
  908.0 10.1 copy.496
  918.1 10.4 bitcast_convert_fusion.2
  928.4 7.7 copy.456
  937.8 29.1 %all_to_all.168 = bf16[8,2,32768]{2,1,0:T(2,128)(2,1)} all-to-all(bf16[8,2,32768]{2,1,0:T(2,128)(2,1)S(1)} %reshape.1024), channel_id=1, replica_groups=mesh['px'=8,'py'=4] {'px'}, dimensions={0} | all-to-all | bytes 2097152 | tf_op jit(solution)/shard_map/all_to_all | solution.py:136
  976.8 8.1 fusion.29
  997.2 28.7 %all_to_all.169 = bf16[8,2,32768]{2,1,0:T(2,128)(2,1)S(1)} all-to-all(bf16[8,2,32768]{2,1,0:T(2,128)(2,1)S(1)} %reshape.1026), channel_id=1, replica_groups=mesh['px'=8,'py'=4] {'px'}, dimensions={0} | all-to-all | bytes 2097152 | tf_op jit(solution)/shard_map/all_to_all | solution.py:150
  1035.1 4.6 copy.470
  1039.8 16.5 %copy.471 = bf16[64,16,128,16]{0,3,1,2:T(8,128)(2,1)} copy(bf16[64,16,128,16]{2,1,3,0:T(8,128)(2,1)} %bitcast.369) | data formatting | bytes 8388608 | tf_op jit(solution)/shard_map/convert_element_type | solution.py:154
  1056.3 9.5 reshape.1028
  1065.8 5.0 all-to-all-start.11
  1072.5 15.5 %fusion.56 = f32[16,32,128,64]{2,3,1,0:T(8,128)} fusion(bf16[64,16,32,128]{3,2,1,0:T(8,128)(2,1)} %copy-done.2, bf16[2,64,64]{2,1,0:T(8,128)(2,1)S(1)} %copy-done.7), kind=kOutput, calls=%fused_computation.111 | convolution fusion | flops 536870912 | bytes 25182208 | tf_op jit(solution)/shard_map/io,ixyz->oxyz/dot_general | solution.py:234
  1088.1 30.9 %all-to-all-done.11 = bf16[4,2,262144]{2,1,0:T(2,128)(2,1)} async-done(((bf16[4,2,262144]{2,1,0:T(2,128)(2,1)}), bf16[4,2,262144]{2,1,0:T(2,128)(2,1)}, u32[]{:S(2)}, u32[]{:S(2)}) %all-to-all-start.11) | async-done | bytes 4194336 | tf_op jit(solution)/shard_map/all_to_all | solution.py:157
  1119.0 9.3 reshape.1029
  1128.3 9.1 copy.473
  1137.4 13.1 copy.474
  1150.5 45.9 %fusion.27 = bf16[64,16,32,128]{3,2,1,0:T(8,128)(2,1)} fusion(f32[16,32,128,64]{2,3,1,0:T(8,128)} %fusion.56, bf16[64,16,32,64]{3,2,1,0:T(8,128)(2,1)} %copy.474, f32[128,64,1,1]{0,1,3,2:T(8,128)S(1)} %bitcast.389, f32[64]{0:T(128)S(1)} %get-tuple-element.224), kind=kOutput, calls=%fused_computation.57 | convolution fusion | flops 3502243840 | bytes 29393152 | tf_op jit(solution)/shard_map/cxyq,qz->cxyz/dot_general | solution.py:158
  1196.3 17.7 %copy.478 = bf16[64,16,32,128]{0,3,2,1:T(8,128)(2,1)} copy(bf16[64,16,32,128]{3,2,1,0:T(8,128)(2,1)} %fusion.27) | data formatting | bytes 16777216 | tf_op jit(solution)/shard_map/convert_element_type | solution.py:239
  1214.0 15.3 %copy.479 = bf16[8,8,8,64,2,4,16]{3,6,5,4,2,1,0:T(8,128)(2,1)} copy(bf16[8,8,8,64,2,4,16]{3,6,2,5,1,4,0:T(8,128)(2,1)} %bitcast.355) | data formatting | bytes 16777216 | tf_op jit(solution)/shard_map/transpose | solution.py:117
  1229.3 26.6 %gather_fusion.4 = bf16[1024,64,128]{1,2,0:T(8,128)(2,1)} fusion(bf16[512,64,128]{1,2,0:T(8,128)(2,1)} %bitcast.353, s32[1024]{0:T(1024)S(1)} %copy-done.3), kind=kCustom, calls=%fused_computation.4 | custom fusion | bytes 33558528 | tf_op jit(solution)/shard_map/jit(_take)/gather | solution.py:241
  1255.9 30.5 %copy.481 = bf16[256,4,64,128]{3,2,1,0:T(8,128)(2,1)} copy(bf16[256,4,64,128]{2,3,1,0:T(8,128)(2,1)} %bitcast.352) | data formatting | bytes 33554432 | tf_op jit(solution)/shard_map/jit(_take)/gather | solution.py:241
  1286.4 22.2 %fusion.55 = bf16[256,64,128]{2,1,0:T(8,128)(2,1)} fusion(bf16[256,4,128,128]{3,2,1,0:T(8,128)(2,1)} %bitcast.394, bf16[256,4,64,128]{3,2,1,0:T(8,128)(2,1)} %copy.481, pred[256,4]{1,0:T(8,128)(4,1)S(1)} %bitcast.390), kind=kOutput, calls=%fused_computation.106 | convolution fusion | flops 2160066560 | bytes 54526976 | tf_op jit(solution)/shard_map/nhcx,nhpx->ncp/dot_general | solution.py:91
  1312.9 93.2 %all-to-all-done.12 = bf16[256,64,128]{2,1,0:T(8,128)(2,1)} async-done(((bf16[256,64,128]{2,1,0:T(8,128)(2,1)}), bf16[256,64,128]{2,1,0:T(8,128)(2,1)}, u32[]{:S(2)}, u32[]{:S(2)}) %all-to-all-start.12) | async-done | bytes 4194336 | tf_op jit(solution)/shard_map/all_to_all | solution.py:182
  1406.1 4.3 gather_fusion.5
  (339 shorter events, 256.3 us)
Async XLA Ops:
  0.0 24.6 %copy-start = (bf16[128,64,128]{2,1,0:T(8,128)(2,1)S(1)}, bf16[128,64,128]{2,1,0:T(8,128)(2,1)}, u32[]{:S(2)}) copy-start(bf16[128,64,128]{2,1,0:T(8,128)(2,1)} %param.9) | copy-start | bytes 6291460
  1.7 0.8 copy-start.9
  5.5 14.4 %all-to-all-start.2 = ((s32[32,8,1]{1,2,0:T(1,128)}), s32[32,8,1]{1,2,0:T(1,128)S(1)}, u32[]{:S(2)}, u32[]{:S(2)}) async-start(s32[32,8,1]{1,2,0:T(1,128)} %bitcast.34), calls=%async_computation.2 | async-start | bytes 32768 | tf_op jit(solution)/shard_map/all_to_all | solution.py:212
  19.9 12.0 all-to-all-start
  31.9 110.6 %copy-start.4 = (s32[32,8,4]{1,2,0:T(4,128)}, s32[32,8,4]{1,2,0:T(4,128)S(1)}, u32[]{:S(2)}) copy-start(s32[32,8,4]{1,2,0:T(4,128)S(1)} %all-to-all-done) | copy-start | bytes 12292
  31.9 13.2 all-to-all-start.1
  45.0 97.5 %all-to-all-start.3 = ((bf16[256,64,128]{2,1,0:T(8,128)(2,1)}), bf16[256,64,128]{2,1,0:T(8,128)(2,1)}, u32[]{:S(2)}, u32[]{:S(2)}) async-start(bf16[256,64,128]{2,1,0:T(8,128)(2,1)} %select_select_fusion), calls=%async_computation.3 | async-start | bytes 8388608 | tf_op jit(solution)/shard_map/all_to_all | solution.py:210
  416.3 53.3 %all-to-all-start.4 = ((bf16[4,2,262144]{2,1,0:T(2,128)(2,1)}), bf16[4,2,262144]{2,1,0:T(2,128)(2,1)}, u32[]{:S(2)}, u32[]{:S(2)}) async-start(bf16[4,2,262144]{2,1,0:T(2,128)(2,1)} %reshape.1014), calls=%async_computation.4 | async-start | bytes 8388608 | tf_op jit(solution)/shard_map/all_to_all | solution.py:128
  619.9 31.2 %copy-start.8 = (f32[2,64]{1,0:T(2,128)S(1)}, f32[2,64]{1,0:T(2,128)}, u32[]{:S(2)}) copy-start(f32[2,64]{1,0:T(2,128)} %param.15) | copy-start | bytes 1540
  619.9 31.2 %copy-start.7 = (bf16[2,64,64]{2,1,0:T(8,128)(2,1)S(1)}, bf16[2,64,64]{2,1,0:T(8,128)(2,1)}, u32[]{:S(2)}) copy-start(bf16[2,64,64]{2,1,0:T(8,128)(2,1)} %param.14) | copy-start | bytes 49156
  646.0 53.2 %all-to-all-start.7 = ((bf16[4,2,262144]{2,1,0:T(2,128)(2,1)}), bf16[4,2,262144]{2,1,0:T(2,128)(2,1)}, u32[]{:S(2)}, u32[]{:S(2)}) async-start(bf16[4,2,262144]{2,1,0:T(2,128)(2,1)} %reshape.1020), calls=%async_computation.7 | async-start | bytes 8388608 | tf_op jit(solution)/shard_map/all_to_all | solution.py:157
  797.7 3.2 copy-start.2
  1039.8 31.0 %copy-start.5 = (s32[32,8,4]{1,2,0:T(4,128)S(1)}, s32[32,8,4]{1,2,0:T(4,128)}, u32[]{:S(2)}) copy-start(s32[32,8,4]{1,2,0:T(4,128)} %copy-done.4) | copy-start | bytes 12292
  1065.8 53.2 %all-to-all-start.11 = ((bf16[4,2,262144]{2,1,0:T(2,128)(2,1)}), bf16[4,2,262144]{2,1,0:T(2,128)(2,1)}, u32[]{:S(2)}, u32[]{:S(2)}) async-start(bf16[4,2,262144]{2,1,0:T(2,128)(2,1)} %reshape.1028), calls=%async_computation.11 | async-start | bytes 8388608 | tf_op jit(solution)/shard_map/all_to_all | solution.py:157
  1214.0 15.3 %copy-start.3 = (s32[1024]{0:T(1024)S(1)}, s32[1024]{0:T(1024)}, u32[]{:S(2)}) copy-start(s32[1024]{0:T(1024)} %broadcast_clamp_fusion) | copy-start | bytes 12292
  1255.9 30.5 %copy-start.6 = (pred[32,8,4]{2,1,0:T(8,128)(4,1)S(1)}, pred[32,8,4]{2,1,0:T(8,128)(4,1)}, u32[]{:S(2)}) copy-start(pred[32,8,4]{2,1,0:T(8,128)(4,1)} %copy.505) | copy-start | bytes 3076
  1286.4 25.8 %copy-start.10 = (s32[128]{0:T(128)S(1)}, s32[128]{0:T(128)}, u32[]{:S(2)}) copy-start(s32[128]{0:T(128)} %copy-done.9) | copy-start | bytes 1540
  1286.4 127.2 %copy-start.1 = (bf16[128,64,128]{2,1,0:T(8,128)(2,1)S(1)}, bf16[128,64,128]{2,1,0:T(8,128)(2,1)}, u32[]{:S(2)}) copy-start(bf16[128,64,128]{2,1,0:T(8,128)(2,1)} %param.9) | copy-start | bytes 6291460
  1308.6 97.5 %all-to-all-start.12 = ((bf16[256,64,128]{2,1,0:T(8,128)(2,1)}), bf16[256,64,128]{2,1,0:T(8,128)(2,1)}, u32[]{:S(2)}, u32[]{:S(2)}) async-start(bf16[256,64,128]{2,1,0:T(8,128)(2,1)} %fusion.55), calls=%async_computation.12 | async-start | bytes 8388608 | tf_op jit(solution)/shard_map/all_to_all | solution.py:182
where the time goes:
time: 1430 us; the launch traced here: 1410 us
  local copies, waits for them, and re-layouts  462 us (32%)
  waiting for transfers between devices  310 us (22%)
  matrix products  273 us (19%)
  blocking collectives  170 us (12%)
  other arithmetic  160 us (11%)
  starting transfers between devices  36.7 us (3%)
    unnamed x39, local copies, waits for them, and re-layouts  97.6 us
    all_to_all x1, waiting for transfers between devices, route_back(): lax.all_to_all(values, ('px', 'py'), split_axis=0, concat_axis=0, tiled=T...  93.2 us
    all_to_all x1, waiting for transfers between devices, per_device(): lax.all_to_all(packed_features, ('px', 'py'), split_axis=0, concat_axis=0...  91.7 us
    dot_general x2, matrix products, spectral(): jnp.einsum('cxyq,qz->cxyz', column_back.astype(jnp.float32), back_third,...  74.5 us
    all_to_all x2, waiting for transfers between devices, spectral(): lax.all_to_all(second_back, 'py', split_axis=2, concat_axis=3, tiled=True)  66.3 us
    reduce_sum x16, other arithmetic, one_group(): distance = jnp.sum(apart * apart, axis=2)  65.9 us
    all_to_all x2, blocking collectives, spectral(): lax.all_to_all(second_modes, 'px', split_axis=3, concat_axis=1, tiled=True)  58.4 us
    all_to_all x2, blocking collectives, spectral(): lax.all_to_all(first_back, 'px', split_axis=1, concat_axis=3, tiled=True)  57.6 us
  transfers between devices with their start and end apart: 8, of which 8 were waited for; matrix products, arithmetic and copies ran while one was open for 3% of the time, Pallas kernels for 0%

commit v1 on v0

--- a/solution.py
+++ b/solution.py
@@ -125,7 +125,10 @@
     third_modes = jnp.einsum(
         "cxyz,zq->cxyq", grid.astype(jnp.float32), table_third, precision=PRECISE
     ).astype(jnp.bfloat16)
-    columns = lax.all_to_all(third_modes, "py", split_axis=3, concat_axis=2, tiled=True)
+    columns = jnp.concatenate(
+        lax.all_to_all(jnp.stack(jnp.split(third_modes, lax.axis_size("py"), axis=3)), "py", 0, 0),
+        axis=2,
+    )
     third_local = columns.shape[3] // 2
     second_modes = jnp.einsum(
         "cxyzp,ypkq->cxzkq",

time: 1430 us -> 1530 us (1.070)
  local copies, waits for them, and re-layouts: 462 us -> 558 us
    another operation x0 -> x12, local copies, waits for them, and re-layouts: none -> 133 us  [the longest x10 113 us: spectral(): jnp.stack(jnp.split(third_modes, lax.axis_size('py'), axis=3))]
    convert_element_type x2 -> x0, local copies, waits for them, and re-layouts: 32.7 us -> none  [spectral(): third_modes = jnp.einsum('cxyz,zq->cxyq', grid.astype(jnp.float32), table...]
    all_to_all x2 -> x0, local copies, waits for them, and re-layouts: 18.5 us -> none  [spectral(): lax.all_to_all(third_modes, 'py', split_axis=3, concat_axis=2, tiled=True)]
    reshape x2 -> x4, local copies, waits for them, and re-layouts: 20.1 us -> 36.7 us  [spectral(): jnp.concatenate(lax.all_to_all(jnp.stack(jnp.split(third_modes, lax.axis_...]
    unnamed x39 -> x43, local copies, waits for them, and re-layouts: 97.6 us -> 94.2 us
where the time goes in v1:
time: 1530 us; the launch traced here: 1520 us
  local copies, waits for them, and re-layouts  558 us (36%)
  waiting for transfers between devices  309 us (20%)
  matrix products  270 us (18%)
  other arithmetic  175 us (11%)
  blocking collectives  170 us (11%)
  starting transfers between devices  36.9 us (2%)
    another operation x10, local copies, waits for them, and re-layouts, spectral(): jnp.stack(jnp.split(third_modes, lax.axis_size('py'), axis=3))  113 us
    unnamed x43, local copies, waits for them, and re-layouts  94.2 us
    all_to_all x1, waiting for transfers between devices, route_back(): lax.all_to_all(values, ('px', 'py'), split_axis=0, concat_axis=0, tiled=T...  93.2 us
    all_to_all x1, waiting for transfers between devices, per_device(): lax.all_to_all(packed_features, ('px', 'py'), split_axis=0, concat_axis=0...  91.2 us
    dot_general x2, matrix products, spectral(): jnp.einsum('cxyq,qz->cxyz', column_back.astype(jnp.float32), back_third,...  74.5 us
    reduce_sum x16, other arithmetic, one_group(): distance = jnp.sum(apart * apart, axis=2)  65.9 us
    all_to_all x2, waiting for transfers between devices, spectral(): lax.all_to_all(second_back, 'py', split_axis=2, concat_axis=3, tiled=True)  65.7 us
    all_to_all x2, blocking collectives, spectral(): lax.all_to_all(second_modes, 'px', split_axis=3, concat_axis=1, tiled=True)  58.1 us
  transfers between devices with their start and end apart: 8, of which 8 were waited for; matrix products, arithmetic and copies ran while one was open for 3% of the time, Pallas kernels for 0%

profile of v1, /device:TPU:0, one launch (start us, length us, event | category | flops | bytes accessed | tf_op | source)
XLA Modules:
  0.0 1520.2 jit_solution(2514492749766168289)
XLA Ops:
  5.5 7.3 all-to-all-start.2
  51.3 91.2 %all-to-all-done.3 = bf16[256,64,128]{2,1,0:T(8,128)(2,1)} async-done(((bf16[256,64,128]{2,1,0:T(8,128)(2,1)}), bf16[256,64,128]{2,1,0:T(8,128)(2,1)}, u32[]{:S(2)}, u32[]{:S(2)}) %all-to-all-start.3) | async-done | bytes 4194336 | tf_op jit(solution)/shard_map/all_to_all | solution.py:213
  142.5 155.0 %while.15 = (s32[]{:T(128)}, bf16[16,16,4,128,128]{4,3,2,1,0:T(8,128)(2,1)}, bf16[16,16,4,64,128]{4,3,2,1,0:T(8,128)(2,1)}, bf16[16,16,3,128]{3,2,1,0:T(4,128)(2...) while((s32[]{:T(128)}, ...), condition=%wide.region_5.6_spmd, body=%wide.region_3.5_spmd.sunk | while | flops 151557504 | bytes 16284649 | solution.py:83
  297.5 30.0 %fusion.59 = bf16[512,64,128]{2,0,1:T(8,128)(2,1)} fusion(bf16[1024,64,128]{2,1,0:T(8,128)(2,1)} %bitcast.409, s32[1024]{0:T(1024)S(1)} %eq.74), kind=kOutput, calls=%fused_computation.126 | convolution fusion | flops 8594653184 | bytes 25169920 | tf_op jit(solution)/shard_map/rb,rcx->bcx/dot_general | solution.py:103
  327.5 17.6 %copy.435 = bf16[512,64,128]{1,2,0:T(8,128)(2,1)} copy(bf16[512,64,128]{2,0,1:T(8,128)(2,1)} %fusion.59) | data formatting | bytes 16777216 | tf_op jit(solution)/shard_map/convert_element_type | solution.py:221
  345.1 15.1 copy.436
  360.2 19.0 %copy.438 = bf16[64,16,32,128]{3,2,1,0:T(8,128)(2,1)} copy(bf16[64,16,32,128]{0,3,2,1:T(8,128)(2,1)} %bitcast.368) | data formatting | bytes 16777216 | tf_op jit(solution)/shard_map/reshape | solution.py:109
  379.2 9.1 convolution_convert_fusion.1
  388.3 13.1 slice_bitcast_fusion.7
  401.4 10.1 copy.439
  411.5 11.1 copy.440
  422.6 11.1 copy.441
  433.7 11.1 copy.442
  452.0 9.5 reshape.1012
  466.9 48.0 %all-to-all-done.4 = bf16[4,2,262144]{2,1,0:T(2,128)(2,1)} async-done(((bf16[4,2,262144]{2,1,0:T(2,128)(2,1)}), bf16[4,2,262144]{2,1,0:T(2,128)(2,1)}, u32[]{:S(2)}, u32[]{:S(2)}) %all-to-all-start.4) | async-done | bytes 4194336 | tf_op jit(solution)/shard_map/all_to_all | solution.py:129
  514.9 9.3 reshape.1013
  524.2 9.2 bitcast_bitcast_fusion.1
  533.4 9.1 copy.443
  542.5 10.1 copy.502
  552.6 10.4 bitcast_convert_fusion.4
  563.0 7.7 copy.445
  572.4 29.0 %all_to_all.145 = bf16[8,2,32768]{2,1,0:T(2,128)(2,1)} all-to-all(bf16[8,2,32768]{2,1,0:T(2,128)(2,1)S(1)} %reshape.1014), channel_id=1, replica_groups=mesh['px'=8,'py'=4] {'px'}, dimensions={0} | all-to-all | bytes 2097152 | tf_op jit(solution)/shard_map/all_to_all | solution.py:139
  611.3 8.1 fusion.32
  631.7 28.9 %all_to_all.146 = bf16[8,2,32768]{2,1,0:T(2,128)(2,1)S(1)} all-to-all(bf16[8,2,32768]{2,1,0:T(2,128)(2,1)S(1)} %reshape.1016), channel_id=1, replica_groups=mesh['px'=8,'py'=4] {'px'}, dimensions={0} | all-to-all | bytes 2097152 | tf_op jit(solution)/shard_map/all_to_all | solution.py:153
  674.4 16.5 %copy.460 = bf16[64,16,128,16]{0,3,1,2:T(8,128)(2,1)} copy(bf16[64,16,128,16]{2,1,3,0:T(8,128)(2,1)} %bitcast.382) | data formatting | bytes 8388608 | tf_op jit(solution)/shard_map/convert_element_type | solution.py:157
  691.0 9.6 reshape.1018
  706.2 12.8 fusion.106
  719.0 34.8 %all-to-all-done.7 = bf16[4,2,262144]{2,1,0:T(2,128)(2,1)} async-done(((bf16[4,2,262144]{2,1,0:T(2,128)(2,1)}), bf16[4,2,262144]{2,1,0:T(2,128)(2,1)}, u32[]{:S(2)}, u32[]{:S(2)}) %all-to-all-start.7) | async-done | bytes 4194336 | tf_op jit(solution)/shard_map/all_to_all | solution.py:160
  753.8 9.3 reshape.1019
  763.1 9.1 copy.462
  772.2 13.1 copy.464
  785.3 28.6 %fusion.54 = (u16[64,32,128]{2,1,0:T(8,128)(2,1)S(1)}, f32[64,16,32,128]{3,2,1,0:T(8,128)}) fusion(f32[64]{0:T(128)S(1)} %get-tuple-element.233, f32[16,32,128,64]{2,3,1,0:T(8,128)} %fusion.106, bf16[64,16,32,64]{3,2,1,0:T(8,128)(2,1)} %copy.464, f32[128,64,1,1]{0,1,3,2:T(8,128)S(1)} %bitcast.402), kind=kOutput, calls=%fused_computation.104 | convolution fusion | flops 3258712064 | bytes 38306048 | tf_op jit(solution)/shard_map/cxyq,qz->cxyz/dot_general | solution.py:161
  813.9 38.4 %fusion.24 = bf16[64,16,32,128]{3,2,1,0:T(8,128)(2,1)S(1)} fusion(f32[64,16,32,128]{3,2,1,0:T(8,128)} %get-tuple-element.238, u16[64,32,128]{2,1,0:T(8,128)(2,1)S(1)} %get-tuple-element.237), kind=kLoop, calls=%fused_computation.54 | loop fusion | flops 285212672 | bytes 25690112 | tf_op jit(solution)/shard_map/convert_element_type | solution.py:242
  859.5 13.2 slice_bitcast_fusion.3
  872.7 10.1 copy.468
  882.8 11.1 copy.469
  893.9 11.1 copy.470
  905.0 11.1 copy.471
  916.0 7.2 fusion.128
  923.3 9.5 reshape.1020
  932.8 54.0 %all_to_all.147 = bf16[4,2,262144]{2,1,0:T(2,128)(2,1)} all-to-all(bf16[4,2,262144]{2,1,0:T(2,128)(2,1)} %reshape.1020), channel_id=1, replica_groups=mesh['px'=8,'py'=4] {'py'}, dimensions={0} | all-to-all | bytes 8388608 | tf_op jit(solution)/shard_map/all_to_all | solution.py:129
  986.8 9.3 reshape.1021
  996.0 9.2 bitcast_bitcast_fusion
  1005.3 9.1 copy.472
  1014.4 10.0 copy.514
  1024.5 10.4 bitcast_convert_fusion.2
  1034.8 7.7 copy.474
  1044.2 29.1 %all_to_all.148 = bf16[8,2,32768]{2,1,0:T(2,128)(2,1)} all-to-all(bf16[8,2,32768]{2,1,0:T(2,128)(2,1)S(1)} %reshape.1022), channel_id=1, replica_groups=mesh['px'=8,'py'=4] {'px'}, dimensions={0} | all-to-all | bytes 2097152 | tf_op jit(solution)/shard_map/all_to_all | solution.py:139
  1083.2 8.1 fusion.29
  1103.6 28.7 %all_to_all.149 = bf16[8,2,32768]{2,1,0:T(2,128)(2,1)S(1)} all-to-all(bf16[8,2,32768]{2,1,0:T(2,128)(2,1)S(1)} %reshape.1024), channel_id=1, replica_groups=mesh['px'=8,'py'=4] {'px'}, dimensions={0} | all-to-all | bytes 2097152 | tf_op jit(solution)/shard_map/all_to_all | solution.py:153
  1146.1 16.5 %copy.489 = bf16[64,16,128,16]{0,3,1,2:T(8,128)(2,1)} copy(bf16[64,16,128,16]{2,1,3,0:T(8,128)(2,1)} %bitcast.383) | data formatting | bytes 8388608 | tf_op jit(solution)/shard_map/convert_element_type | solution.py:157
  1162.6 9.5 reshape.1026
  1178.9 15.5 %fusion.56 = f32[16,32,128,64]{2,3,1,0:T(8,128)} fusion(bf16[64,16,32,128]{3,2,1,0:T(8,128)(2,1)} %copy-done.2, bf16[2,64,64]{2,1,0:T(8,128)(2,1)S(1)} %copy-done.8), kind=kOutput, calls=%fused_computation.121 | convolution fusion | flops 536870912 | bytes 25182208 | tf_op jit(solution)/shard_map/io,ixyz->oxyz/dot_general | solution.py:237
  1194.4 30.9 %all-to-all-done.11 = bf16[4,2,262144]{2,1,0:T(2,128)(2,1)} async-done(((bf16[4,2,262144]{2,1,0:T(2,128)(2,1)}), bf16[4,2,262144]{2,1,0:T(2,128)(2,1)}, u32[]{:S(2)}, u32[]{:S(2)}) %all-to-all-start.11) | async-done | bytes 4194336 | tf_op jit(solution)/shard_map/all_to_all | solution.py:160
  1225.3 9.3 reshape.1027
  1234.7 9.1 copy.491
  1243.8 13.1 copy.492
  1256.9 45.9 %fusion.27 = bf16[64,16,32,128]{3,2,1,0:T(8,128)(2,1)} fusion(f32[16,32,128,64]{2,3,1,0:T(8,128)} %fusion.56, bf16[64,16,32,64]{3,2,1,0:T(8,128)(2,1)} %copy.492, f32[128,64,1,1]{0,1,3,2:T(8,128)S(1)} %bitcast.403, f32[64]{0:T(128)S(1)} %copy-done.12), kind=kOutput, calls=%fused_computation.57 | convolution fusion | flops 3502243840 | bytes 29393152 | tf_op jit(solution)/shard_map/cxyq,qz->cxyz/dot_general | solution.py:161
  1302.8 17.7 %copy.496 = bf16[64,16,32,128]{0,3,2,1:T(8,128)(2,1)} copy(bf16[64,16,32,128]{3,2,1,0:T(8,128)(2,1)} %fusion.27) | data formatting | bytes 16777216 | tf_op jit(solution)/shard_map/convert_element_type | solution.py:242
  1320.4 15.3 %copy.497 = bf16[8,8,8,64,2,4,16]{3,6,5,4,2,1,0:T(8,128)(2,1)} copy(bf16[8,8,8,64,2,4,16]{3,6,2,5,1,4,0:T(8,128)(2,1)} %bitcast.373) | data formatting | bytes 16777216 | tf_op jit(solution)/shard_map/transpose | solution.py:117
  1335.8 26.7 %gather_fusion.4 = bf16[1024,64,128]{1,2,0:T(8,128)(2,1)} fusion(bf16[512,64,128]{1,2,0:T(8,128)(2,1)} %bitcast.371, s32[1024]{0:T(1024)S(1)} %copy-done.3), kind=kCustom, calls=%fused_computation.4 | custom fusion | bytes 33558528 | tf_op jit(solution)/shard_map/jit(_take)/gather | solution.py:244
  1362.4 30.4 %copy.499 = bf16[256,4,64,128]{3,2,1,0:T(8,128)(2,1)} copy(bf16[256,4,64,128]{2,3,1,0:T(8,128)(2,1)} %bitcast.370) | data formatting | bytes 33554432 | tf_op jit(solution)/shard_map/jit(_take)/gather | solution.py:244
  1392.8 22.2 %fusion.55 = bf16[256,64,128]{2,1,0:T(8,128)(2,1)} fusion(bf16[256,4,128,128]{3,2,1,0:T(8,128)(2,1)} %bitcast.408, bf16[256,4,64,128]{3,2,1,0:T(8,128)(2,1)} %copy.499, pred[256,4]{1,0:T(8,128)(4,1)S(1)} %bitcast.404), kind=kOutput, calls=%fused_computation.116 | convolution fusion | flops 2160066560 | bytes 54526976 | tf_op jit(solution)/shard_map/nhcx,nhpx->ncp/dot_general | solution.py:91
  1419.4 93.2 %all-to-all-done.12 = bf16[256,64,128]{2,1,0:T(8,128)(2,1)} async-done(((bf16[256,64,128]{2,1,0:T(8,128)(2,1)}), bf16[256,64,128]{2,1,0:T(8,128)(2,1)}, u32[]{:S(2)}, u32[]{:S(2)}) %all-to-all-start.12) | async-done | bytes 4194336 | tf_op jit(solution)/shard_map/all_to_all | solution.py:185
  (355 shorter events, 317.1 us)
Async XLA Ops:
  0.0 24.6 %copy-start = (bf16[128,64,128]{2,1,0:T(8,128)(2,1)S(1)}, bf16[128,64,128]{2,1,0:T(8,128)(2,1)}, u32[]{:S(2)}) copy-start(bf16[128,64,128]{2,1,0:T(8,128)(2,1)} %param.9) | copy-start | bytes 6291460
  1.7 0.8 copy-start.10
  5.5 14.4 all-to-all-start.2
  19.9 11.9 all-to-all-start
  31.9 110.6 %copy-start.4 = (s32[32,8,4]{1,2,0:T(4,128)}, s32[32,8,4]{1,2,0:T(4,128)S(1)}, u32[]{:S(2)}) copy-start(s32[32,8,4]{1,2,0:T(4,128)S(1)} %all-to-all-done) | copy-start | bytes 12292
  31.9 13.2 all-to-all-start.1
  45.0 97.5 %all-to-all-start.3 = ((bf16[256,64,128]{2,1,0:T(8,128)(2,1)}), bf16[256,64,128]{2,1,0:T(8,128)(2,1)}, u32[]{:S(2)}, u32[]{:S(2)}) async-start(bf16[256,64,128]{2,1,0:T(8,128)(2,1)} %select_select_fusion), calls=%async_computation.3 | async-start | bytes 8388608 | tf_op jit(solution)/shard_map/all_to_all | solution.py:213
  461.5 53.5 %all-to-all-start.4 = ((bf16[4,2,262144]{2,1,0:T(2,128)(2,1)}), bf16[4,2,262144]{2,1,0:T(2,128)(2,1)}, u32[]{:S(2)}, u32[]{:S(2)}) async-start(bf16[4,2,262144]{2,1,0:T(2,128)(2,1)} %reshape.1012), calls=%async_computation.4 | async-start | bytes 8388608 | tf_op jit(solution)/shard_map/all_to_all | solution.py:129
  674.4 31.2 %copy-start.6 = (f32[128,32,2]{0,1,2:T(8,128)S(1)}, f32[128,32,2]{0,1,2:T(8,128)}, u32[]{:S(2)}) copy-start(f32[128,32,2]{0,1,2:T(8,128)} %get-tuple-element.228) | copy-start | bytes 98308
  674.4 31.2 %copy-start.9 = (f32[2,64]{1,0:T(2,128)S(1)}, f32[2,64]{1,0:T(2,128)}, u32[]{:S(2)}) copy-start(f32[2,64]{1,0:T(2,128)} %param.15) | copy-start | bytes 1540
  674.4 31.8 %copy-start.8 = (bf16[2,64,64]{2,1,0:T(8,128)(2,1)S(1)}, bf16[2,64,64]{2,1,0:T(8,128)(2,1)}, u32[]{:S(2)}) copy-start(bf16[2,64,64]{2,1,0:T(8,128)(2,1)} %param.14) | copy-start | bytes 49156
  700.5 53.2 %all-to-all-start.7 = ((bf16[4,2,262144]{2,1,0:T(2,128)(2,1)}), bf16[4,2,262144]{2,1,0:T(2,128)(2,1)}, u32[]{:S(2)}, u32[]{:S(2)}) async-start(bf16[4,2,262144]{2,1,0:T(2,128)(2,1)} %reshape.1018), calls=%async_computation.7 | async-start | bytes 8388608 | tf_op jit(solution)/shard_map/all_to_all | solution.py:160
  852.3 20.5 %copy-start.2 = (bf16[64,16,32,128]{3,2,1,0:T(8,128)(2,1)}, bf16[64,16,32,128]{3,2,1,0:T(8,128)(2,1)S(1)}, u32[]{:S(2)}) copy-start(bf16[64,16,32,128]{3,2,1,0:T(8,128)(2,1)S(1)} %fusion.24) | copy-start | bytes 25165828
  1146.1 31.0 %copy-start.5 = (s32[32,8,4]{1,2,0:T(4,128)S(1)}, s32[32,8,4]{1,2,0:T(4,128)}, u32[]{:S(2)}) copy-start(s32[32,8,4]{1,2,0:T(4,128)} %copy-done.4) | copy-start | bytes 12292
  1172.1 53.2 %all-to-all-start.11 = ((bf16[4,2,262144]{2,1,0:T(2,128)(2,1)}), bf16[4,2,262144]{2,1,0:T(2,128)(2,1)}, u32[]{:S(2)}, u32[]{:S(2)}) async-start(bf16[4,2,262144]{2,1,0:T(2,128)(2,1)} %reshape.1026), calls=%async_computation.11 | async-start | bytes 8388608 | tf_op jit(solution)/shard_map/all_to_all | solution.py:160
  1234.7 22.3 %copy-start.12 = (f32[64]{0:T(128)S(1)}, f32[64]{0:T(128)}, u32[]{:S(2)}) copy-start(f32[64]{0:T(128)} %get-tuple-element.232) | copy-start | bytes 772
  1320.4 15.3 %copy-start.3 = (s32[1024]{0:T(1024)S(1)}, s32[1024]{0:T(1024)}, u32[]{:S(2)}) copy-start(s32[1024]{0:T(1024)} %broadcast_clamp_fusion) | copy-start | bytes 12292
  1362.4 30.4 %copy-start.7 = (pred[32,8,4]{2,1,0:T(8,128)(4,1)S(1)}, pred[32,8,4]{2,1,0:T(8,128)(4,1)}, u32[]{:S(2)}) copy-start(pred[32,8,4]{2,1,0:T(8,128)(4,1)} %copy.523) | copy-start | bytes 3076
  1392.8 25.8 %copy-start.11 = (s32[128]{0:T(128)S(1)}, s32[128]{0:T(128)}, u32[]{:S(2)}) copy-start(s32[128]{0:T(128)} %copy-done.10) | copy-start | bytes 1540
  1392.8 127.2 %copy-start.1 = (bf16[128,64,128]{2,1,0:T(8,128)(2,1)S(1)}, bf16[128,64,128]{2,1,0:T(8,128)(2,1)}, u32[]{:S(2)}) copy-start(bf16[128,64,128]{2,1,0:T(8,128)(2,1)} %param.9) | copy-start | bytes 6291460
  1415.1 97.5 %all-to-all-start.12 = ((bf16[256,64,128]{2,1,0:T(8,128)(2,1)}), bf16[256,64,128]{2,1,0:T(8,128)(2,1)}, u32[]{:S(2)}, u32[]{:S(2)}) async-start(bf16[256,64,128]{2,1,0:T(8,128)(2,1)} %fusion.55), calls=%async_computation.12 | async-start | bytes 8388608 | tf_op jit(solution)/shard_map/all_to_all | solution.py:185
